TPU v7x, 32 devices: a whole 2x2x4 slice. The times are simulated.
32 devices in a mesh: layer: 4 (over y, x), expert: 4 (over z), dp: 2 (over core).
Axes of the slice: x: 2, y: 2, z: 4, core: 2. Of those that a mesh axis runs over, the one named last changes fastest.
Arguments:
- tokens: bfloat16 [2048, 2304], P(('expert', 'dp')), may hold values from -6 to 6
- expert_ids: int32 [2048], P(('expert', 'dp')), may hold values from 0 to 3, as said below
- slot_ids: int32 [2048], P(('expert', 'dp')), may hold values from 0 to 127, as said below
- live_mask: int32 [2048], P(('expert', 'dp')), may hold values from 0 to 1
- w_enc: bfloat16 [4, 2304, 2048], P('expert', None, 'layer'), may hold values from -0.125 to 0.125
- b_enc: float32 [4, 2048], P('expert', 'layer'), may hold values from -3 to 3
- w_dec: bfloat16 [2, 4, 2048, 2304], P(None, 'expert', 'layer'), may hold values from -0.125 to 0.125
- b_dec: float32 [2, 2304], P(None, 'layer'), may hold values from -3 to 3
- targets: bfloat16 [2, 2048, 2304], P(None, ('expert', 'dp'), 'layer'), may hold values from -6 to 6
Outputs:
- recon: bfloat16 [2, 2048, 2304], P(None, ('expert', 'dp'), 'layer')
- grad_w_enc: bfloat16 [4, 2304, 2048], P('expert', 'dp', 'layer')
- grad_b_enc: float32 [4, 2048], P('expert', ('layer', 'dp'))
- grad_w_dec: bfloat16 [2, 4, 2048, 2304], P(None, 'expert', 'layer', 'dp')
- grad_b_dec: float32 [2, 2304], P(None, 'layer')
Inputs may be any that keep to these rules, and one draw needn't show every extreme that they name: `expert_ids`: the 256 tokens of one block name any expert at most 128 times; in every draw one expert is named exactly 128 times by every block. `slot_ids`: tokens of one block that name the same expert have distinct slots.
All inputs are finite; a program needn't handle non-finite values.
Results may differ from a plain program's by a relative error of at most 0.01.
Values may be sent and summed in bfloat16 or wider, within the bound.
A program may use at most 128 MiB of HBM per device.

v0:
```python
import math

import jax
import jax.numpy as jnp
from jax import lax
from jax.sharding import PartitionSpec as P


def place_rows(values, cell_index, total_cells):
    shape = values.shape[:-2] + (total_cells, values.shape[-1])
    zero_fill = jnp.zeros(shape, values.dtype)
    return zero_fill.at[..., cell_index, :].set(values)


def local(tokens, expert_ids, slot_ids, live_mask, w_enc, b_enc, w_dec, b_dec, targets):
    n_expert = lax.axis_size("expert")
    n_layer = lax.axis_size("layer")
    tok_rows, model_width = tokens.shape
    capacity = 2 * tok_rows // n_expert
    total_cells = n_expert * capacity
    cell_index = expert_ids * capacity + slot_ids
    quarter = model_width // n_layer
    targets_count = w_dec.shape[0]
    enc_weight = w_enc[0]
    dec_weight = w_dec[:, 0]
    outgoing = place_rows(tokens, cell_index, total_cells).reshape(n_expert, capacity, model_width)
    arrived = lax.all_to_all(outgoing, "expert", split_axis=0, concat_axis=0, tiled=True).reshape(
        total_cells, model_width
    )
    pre_act = jnp.dot(arrived, enc_weight, preferred_element_type=jnp.float32)
    pre_act = pre_act + b_enc[0][None, :]
    active = jnp.maximum(pre_act, 0.0)
    latents = (active * active).astype(jnp.bfloat16)
    partials = jnp.einsum(
        "rl,tld->trd", latents, dec_weight, preferred_element_type=jnp.float32
    ).astype(jnp.bfloat16)
    summed = lax.psum_scatter(
        lax.optimization_barrier(partials).astype(jnp.float32).astype(jnp.bfloat16),
        "layer",
        scatter_dimension=2,
        tiled=True,
    )
    outgoing_rec = summed.reshape(targets_count, n_expert, capacity, quarter)
    returned = lax.all_to_all(outgoing_rec, "expert", split_axis=1, concat_axis=1, tiled=True)
    recon_sum = returned.reshape(targets_count, total_cells, quarter)[:, cell_index, :]
    recon_full = lax.optimization_barrier(recon_sum).astype(jnp.float32) + b_dec[:, None, :]
    recon = recon_full.astype(jnp.bfloat16)
    coef = 2.0 / math.sqrt(tok_rows)
    live_wide = live_mask.astype(jnp.float32)
    error_grad = (
        coef * live_wide[None, :, None] * (recon_full - targets.astype(jnp.float32))
    ).astype(jnp.bfloat16)
    error_wide = lax.optimization_barrier(error_grad).astype(jnp.float32)
    grad_b_dec = lax.psum(jnp.sum(error_wide, axis=1), ("expert", "dp"))
    outgoing_grad = place_rows(error_grad, cell_index, total_cells).reshape(
        targets_count, n_expert, capacity, quarter
    )
    error_part = lax.all_to_all(
        outgoing_grad, "expert", split_axis=1, concat_axis=1, tiled=True
    ).reshape(targets_count, total_cells, quarter)
    segment = lax.all_gather(error_part, "layer", axis=2, tiled=True)
    block_grad = jnp.einsum("rl,trd->tld", latents, segment, preferred_element_type=jnp.float32)
    grad_lat_acc = jnp.einsum(
        "trd,tld->rl", segment, dec_weight, preferred_element_type=jnp.float32
    )
    grad_pre = (grad_lat_acc * (2.0 * active)).astype(jnp.bfloat16)
    grad_enc = jnp.einsum("rd,rl->dl", arrived, grad_pre, preferred_element_type=jnp.float32)
    grad_bias = jnp.sum(lax.optimization_barrier(grad_pre).astype(jnp.float32), axis=0)
    enc_share, dec_share, bias_share = (
        lax.psum_scatter(
            grad_enc[None].astype(jnp.bfloat16), "dp", scatter_dimension=1, tiled=True
        ).astype(jnp.float32),
        lax.psum_scatter(
            block_grad[:, None].astype(jnp.bfloat16), "dp", scatter_dimension=3, tiled=True
        ).astype(jnp.float32),
        lax.psum_scatter(
            grad_bias[None].astype(jnp.bfloat16), "dp", scatter_dimension=1, tiled=True
        ).astype(jnp.float32),
    )
    return (
        recon,
        enc_share.astype(jnp.bfloat16),
        bias_share,
        dec_share.astype(jnp.bfloat16),
        grad_b_dec,
    )


def solution(mesh):
    placed = (
        P(("expert", "dp"), None),
        P(("expert", "dp")),
        P(("expert", "dp")),
        P(("expert", "dp")),
        P("expert", None, "layer"),
        P("expert", "layer"),
        P(None, "expert", "layer", None),
        P(None, "layer"),
        P(None, ("expert", "dp"), "layer"),
    )
    return jax.shard_map(
        local,
        mesh=mesh,
        in_specs=placed,
        out_specs=(
            P(None, ("expert", "dp"), "layer"),
            P("expert", "dp", "layer"),
            P("expert", ("layer", "dp")),
            P(None, "expert", "layer", "dp"),
            P(None, "layer"),
        ),
        check_vma=False,
    )
```

profile of v0, /device:TPU:0, one launch (start us, length us, event | category | flops | bytes accessed | tf_op | source)
XLA Modules:
  0.0 428.5 jit_solution(17925462820377808188)
XLA Ops:
  7.2 0.0 copy-start
  7.2 0.0 all-reduce.3.cloned.1.call-start
  7.2 0.9 compare_select_fusion
  8.1 4.7 %scatter_custom_fusion = bf16[512,2304]{1,0:T(8,128)(2,1)} fusion(s32[256]{0:T(256)S(1)} %compare_select_fusion, bf16[256,2304]{1,0:T(8,128)(2,1)} %param.9, bf16[]{:T(256)} %constant.7.clone.1), kind=kCustom, calls=%fused_computation.24 | custom fusion | bytes 2359808 | tf_op jit(solution)/shard_map/scatter | solution.py:12
  12.8 0.0 copy-start.3
  12.8 0.0 slice-start
  12.8 60.4 %all_to_all.15 = bf16[4,128,2304]{2,1,0:T(8,128)(2,1)S(1)} all-to-all(bf16[4,128,2304]{2,1,0:T(8,128)(2,1)} %bitcast.59), channel_id=1, replica_groups=mesh['layer'=4,'expert'=4,'dp'=2] {'expert'}, dimensions={0} | all-to-all | bytes 4718592 | tf_op jit(solution)/shard_map/all_to_all | solution.py:27
  73.3 0.0 copy-start.1
  73.3 1.4 copy-done.1
  74.7 0.0 copy-done
  74.7 0.0 copy-done.3
  74.7 0.0 slice-start.1
  74.7 1.4 fusion.18
  76.1 0.0 copy-start.5
  76.1 0.9 copy-done.5
  77.0 0.0 slice-done
  77.0 0.0 slice-done.1
  77.0 4.3 %fusion = bf16[2,512,2304]{2,1,0:T(8,128)(2,1)} fusion(bf16[2,1,512,2304]{3,2,1,0:T(8,128)(2,1)S(1)} %bitcast.68, f32[512,512]{1,0:T(8,128)S(1)} %fusion.18), kind=kOutput, calls=%fused_computation.5 | convolution fusion | flops 2418802688 | bytes 10485760 | tf_op jit(solution)/shard_map/rl,tld->trd/dot_general | solution.py:34
  81.4 12.4 %copy.22 = bf16[2,512,2304]{1,0,2:T(2,128)(2,1)} copy(bf16[2,512,2304]{2,1,0:T(8,128)(2,1)} %fusion) | data formatting | bytes 9437184 | tf_op jit(solution)/shard_map/optimization_barrier | solution.py:38
  93.7 0.0 copy-start.4
  93.7 0.0 all-reduce.3.cloned.1.call-update
  93.8 0.6 copy-done.4
  94.4 0.6 dynamic-slice
  95.6 109.8 %all-reduce.3.cloned.1.call-done = bf16[2,512,2304]{1,0,2:T(2,128)(2,1)} async-done(((bf16[2,512,2304]{1,0,2:T(2,128)(2,1)}), bf16[2,512,2304]{1,0,2:T(2,128)(2,1)}) %all-reduce.3.cloned.1.call-update) | async-done | bytes 4718608
  205.4 2.1 constant_dynamic-slice_fusion
  207.5 1.6 reshape.44
  209.1 2.4 copy.23
  211.6 4.6 %all-to-all-start.1 = ((bf16[2,4,128,576]{2,3,0,1:T(8,128)(2,1)}), bf16[2,4,128,576]{2,3,0,1:T(8,128)(2,1)S(1)}, u32[]{:S(2)}, u32[]{:S(2)}) async-start(bf16[2,4,128,576]{2,3,0,1:T(8,128)(2,1)} %copy.23), calls=%async_computation.1 | async-start | bytes 2359296 | tf_op jit(solution)/shard_map/all_to_all | solution.py:44
  216.2 0.0 copy-start.2
  216.2 0.0 all-gather.2.cloned.1.call-start
  216.2 2.9 copy.25
  219.0 1.2 convert_multiply_fusion
  220.3 24.2 %all-to-all-done.1 = bf16[2,4,128,576]{2,3,0,1:T(8,128)(2,1)S(1)} async-done(((bf16[2,4,128,576]{2,3,0,1:T(8,128)(2,1)}), bf16[2,4,128,576]{2,3,0,1:T(8,128)(2,1)S(1)}, u32[]{:S(2)}, u32[]{:S(2)}) %all-to-all-start.1) | async-done | bytes 1179680 | tf_op jit(solution)/shard_map/all_to_all | solution.py:44
  244.5 3.0 copy.24
  247.5 4.2 gather_fusion
  251.7 0.0 copy-done.2
  251.7 3.3 multiply_convert_fusion
  254.9 1.7 broadcast_in_dim.8
  256.7 27.2 %scatter_fusion = bf16[2,512,576]{2,0,1:T(2,128)(2,1)} fusion(bf16[2,512,576]{2,0,1:T(2,128)(2,1)} %broadcast_in_dim.8, s32[256]{0:T(256)S(1)} %compare_select_fusion, bf16[256,2,576]{2,1,0:T(2,128)(2,1)S(1)} %bitcast.61), kind=kCustom, calls=%fused_computation.2 | custom fusion | bytes 1770496 | tf_op jit(solution)/shard_map/scatter | solution.py:12
  283.8 4.2 copy.26
  288.0 31.5 %all_to_all.16 = bf16[2,4,128,576]{2,3,0,1:T(8,128)(2,1)S(1)} all-to-all(bf16[2,4,128,576]{2,3,0,1:T(8,128)(2,1)} %copy.26), channel_id=1, replica_groups=mesh['layer'=4,'expert'=4,'dp'=2] {'expert'}, dimensions={1} | all-to-all | bytes 2359296 | tf_op jit(solution)/shard_map/all_to_all | solution.py:58
  319.5 1.1 copy_bitcast_fusion
  320.7 0.0 all-gather.2.cloned.1.call-update
  320.7 0.2 reduce-scatter.10.cloned.1.call-start
  320.9 55.0 %all-gather.2.cloned.1.call-done = bf16[2,512,2304]{1,2,0:T(8,128)(2,1)} async-done(((bf16[2,512,576]{1,2,0:T(8,128)(2,1)}), bf16[2,512,2304]{1,2,0:T(8,128)(2,1)}) %all-gather.2.cloned.1.call-update) | async-done | bytes 4718608 | tf_op jit(solution)/shard_map/all_gather | solution.py:61
  375.9 6.6 %fusion.21 = bf16[512,512]{1,0:T(8,128)(2,1)S(1)} fusion(bf16[2,512,2304]{1,2,0:T(8,128)(2,1)} %all-gather.2.cloned.1.call-done, bf16[2,1,512,2304]{3,2,1,0:T(8,128)(2,1)} %param.15, f32[512,512]{1,0:T(8,128)} %copy-done.5), kind=kOutput, calls=%fused_computation.22 | convolution fusion | flops 2416705536 | bytes 11010048 | tf_op jit(solution)/shard_map/trd,tld->rl/dot_general | solution.py:63
  382.6 0.1 reduce_sum.21
  382.7 0.8 reshape_bitcast_fusion
  383.4 0.0 reduce-scatter.10.cloned.1.call-update
  383.5 0.0 reduce-scatter.8.cloned.1.call-start
  383.5 7.4 %fusion.1 = bf16[2,1,512,2304]{2,3,0,1:T(8,128)(2,1)} fusion(bf16[2,512,2304]{1,2,0:T(8,128)(2,1)} %all-gather.2.cloned.1.call-done, f32[512,512]{1,0:T(8,128)} %copy-done.5), kind=kOutput, calls=%fused_computation.6 | convolution fusion | flops 2418802688 | bytes 10485760 | tf_op jit(solution)/shard_map/rl,trd->tld/dot_general | solution.py:62
  390.9 0.0 reduce-scatter.8.cloned.1.call-update
  390.9 0.0 reduce-scatter.6.cloned.1.call-start
  391.0 4.6 %fusion.5 = bf16[1,2304,512]{2,1,0:T(8,128)(2,1)} fusion(bf16[512,2304]{1,0:T(8,128)(2,1)} %bitcast.65, bf16[512,512]{1,0:T(8,128)(2,1)S(1)} %fusion.21), kind=kOutput, calls=%fused_computation.11 | convolution fusion | flops 1209139200 | bytes 5242880 | tf_op jit(solution)/shard_map/rd,rl->dl/dot_general | solution.py:67
  395.5 0.0 reduce-scatter.6.cloned.1.call-update
  395.6 2.9 copy.28
  398.5 0.6 convert_reduce_fusion
  399.1 17.0 %psum.7 = f32[2,576]{1,0:T(2,128)} all-reduce(f32[2,576]{1,0:T(2,128)S(1)} %convert_reduce_fusion), channel_id=1, replica_groups=mesh['layer'=4,'expert'=4,'dp'=2] {'expert','dp'}, use_global_device_ids=true, to_apply=%region_8.0 | all-reduce | flops 1152 | bytes 9216 | tf_op jit(solution)/shard_map/psum | solution.py:54
  416.1 0.0 reduce-scatter.10.cloned.1.call-done
  416.1 0.9 copy.31
  417.1 0.6 convert_element_type.79
  417.7 0.0 reduce-scatter.8.cloned.1.call-done
  417.7 4.3 %copy.29 = bf16[2,1,512,1152]{3,2,1,0:T(8,128)(2,1)} copy(bf16[2,1,512,1152]{2,3,0,1:T(8,128)(2,1)} %reduce-scatter.8.cloned.1.call-done) | data formatting | bytes 4718592
  422.0 0.0 reduce-scatter.6.cloned.1.call-done
  (2 shorter events, 0.0 us)
Async XLA Ops:
  7.2 67.5 %copy-start = (bf16[1,2304,512]{2,1,0:T(8,128)(2,1)S(1)}, bf16[1,2304,512]{2,1,0:T(8,128)(2,1)}, u32[]{:S(2)}) copy-start(bf16[1,2304,512]{2,1,0:T(8,128)(2,1)} %param.13) | copy-start | bytes 7077892
  7.2 198.3 %all-reduce.3.cloned.1.call-start = ((), (), s32[]{:S(2)}) async-start(), calls=%async_computation.10 | async-start | bytes 9437184
  12.8 61.8 %copy-start.3 = (f32[1,512]{1,0:T(1,128)S(1)}, f32[1,512]{1,0:T(1,128)}, u32[]{:S(2)}) copy-start(f32[1,512]{1,0:T(1,128)} %param.14) | copy-start | bytes 6148
  12.8 64.2 %slice-start = ((s8[4718592]{0:T(1024)(128)(4,1)}), s8[4194304]{0:T(1024)(128)(4,1)S(1)}, s32[]{:S(2)}) async-start(s8[4718592]{0:T(1024)(128)(4,1)} %bitcast.67), calls=%async_computation.11 | async-start | bytes 8388608
  73.3 1.4 copy-start.1
  74.7 2.4 slice-start.1
  76.1 1.0 copy-start.5
  93.7 0.7 copy-start.4
  211.6 33.0 %all-to-all-start.1 = ((bf16[2,4,128,576]{2,3,0,1:T(8,128)(2,1)}), bf16[2,4,128,576]{2,3,0,1:T(8,128)(2,1)S(1)}, u32[]{:S(2)}, u32[]{:S(2)}) async-start(bf16[2,4,128,576]{2,3,0,1:T(8,128)(2,1)} %copy.23), calls=%async_computation.1 | async-start | bytes 2359296 | tf_op jit(solution)/shard_map/all_to_all | solution.py:44
  216.2 35.5 %copy-start.2 = (f32[2,576]{1,0:T(2,128)S(1)}, f32[2,576]{1,0:T(2,128)}, u32[]{:S(2)}) copy-start(f32[2,576]{1,0:T(2,128)} %param.16) | copy-start | bytes 13828
  216.2 159.8 %all-gather.2.cloned.1.call-start = ((), (), s32[]{:S(2)}) async-start(), calls=%async_computation.6 | async-start | bytes 5898240 | tf_op jit(solution)/shard_map/all_gather | solution.py:61
  320.7 95.4 %reduce-scatter.10.cloned.1.call-start = ((), (), s32[]{:S(2)}) async-start(), calls=%async_computation.9 | async-start | bytes 196608
  383.5 34.2 %reduce-scatter.8.cloned.1.call-start = ((), (), s32[]{:S(2)}) async-start(), calls=%async_computation.8 | async-start | bytes 7077888 | tf_op jit(solution)/shard_map/reduce_scatter | solution.py:73
  390.9 31.0 %reduce-scatter.6.cloned.1.call-start = ((), (), s32[]{:S(2)}) async-start(), calls=%async_computation.7 | async-start | bytes 3538944 | tf_op jit(solution)/shard_map/reduce_scatter | solution.py:70
Sparse Core Ops, SparseCore 0:
  93.9 111.4 all-reduce.2
  320.8 55.0 all-gather.1
  383.6 7.5 reduce-scatter.9
  393.4 13.6 reduce-scatter.7
  409.7 11.3 reduce-scatter.5
where the time goes:
time: 430 us; the launch traced here: 429 us
  waiting for transfers between devices  189 us (44%)
  blocking collectives  109 us (25%)
  local copies, waits for them, and re-layouts  80 us (19%)
  matrix products  24.3 us (6%)
  between operations  14.5 us (3%)
  other arithmetic  6.69 us (2%)
  starting transfers between devices  4.94 us (1%)
    unnamed x7, waiting for transfers between devices  110 us
    all_to_all x1, blocking collectives, local(): lax.all_to_all(outgoing, 'expert', split_axis=0, concat_axis=0, tiled=True)  60.4 us
    all_gather x1, waiting for transfers between devices, local(): segment = lax.all_gather(error_part, 'layer', axis=2, tiled=True)  55 us
    scatter x2, local copies, waits for them, and re-layouts, place_rows(): return zero_fill.at[..., cell_index, :].set(values)  31.9 us
    all_to_all x1, blocking collectives, local(): lax.all_to_all(outgoing_grad, 'expert', split_axis=1, concat_axis=1, tile...  31.5 us
    all_to_all x1, waiting for transfers between devices, local(): lax.all_to_all(outgoing_rec, 'expert', split_axis=1, concat_axis=1, tiled...  24.2 us
    unnamed x23, local copies, waits for them, and re-layouts  17.5 us
    psum x1, blocking collectives, local(): grad_b_dec = lax.psum(jnp.sum(error_wide, axis=1), ('expert', 'dp'))  17 us
  transfers between devices with their start and end apart: 6, of which 3 were waited for; matrix products, arithmetic and copies ran while one was open for 6% of the time, Pallas kernels for 0%

commit v1 on v0

v1 whole, which is shorter than its diff:
```python
import math

import jax
import jax.numpy as jnp
from jax import lax
from jax.sharding import PartitionSpec as P


def local(tokens, expert_ids, slot_ids, live_mask, w_enc, b_enc, w_dec, b_dec, targets):
    f32, bf16 = jnp.float32, jnp.bfloat16
    n_expert = lax.axis_size("expert")
    n_layer = lax.axis_size("layer")
    n_dp = lax.axis_size("dp")
    tok_rows, model_width = tokens.shape
    capacity = 2 * tok_rows // n_expert
    total_cells = n_expert * capacity
    cell_index = expert_ids * capacity + slot_ids
    quarter = model_width // n_layer
    targets_count = w_dec.shape[0]
    enc_weight = w_enc[0]
    place = (
        lax.broadcasted_iota(jnp.int32, (total_cells, tok_rows), 0) == cell_index[None, :]
    ).astype(bf16)

    cells = lax.dot_general(
        tokens, place, (((0,), (1,)), ((), ())), preferred_element_type=f32
    ).astype(bf16)
    own = lax.dynamic_slice_in_dim(cells, lax.axis_index("layer") * quarter, quarter, 0)
    arrived_part = lax.all_to_all(own, "expert", split_axis=1, concat_axis=1, tiled=True)
    arrived = lax.all_gather(arrived_part, "layer", axis=0, tiled=True)
    pre_act = jnp.einsum("dr,dl->rl", arrived, enc_weight, preferred_element_type=f32)
    pre_act = pre_act + b_enc[0][None, :]
    active = jnp.maximum(pre_act, 0.0)
    latents = (active * active).astype(bf16)

    coef = 2.0 / math.sqrt(tok_rows)
    live_wide = live_mask.astype(f32)
    partials = [
        jnp.einsum("ld,rl->dr", w_dec[t, 0], latents, preferred_element_type=f32).astype(bf16)
        for t in range(targets_count)
    ]
    summed = [
        lax.psum_scatter(p, "layer", scatter_dimension=0, tiled=True) for p in partials
    ]
    recons, errors, segments = [], [], []
    for t in range(targets_count):
        returned = lax.all_to_all(summed[t], "expert", split_axis=1, concat_axis=1, tiled=True)
        recon_sum = jnp.einsum("dr,ri->di", returned, place, preferred_element_type=f32)
        recon_full = recon_sum + b_dec[t][:, None]
        recons.append(recon_full.astype(bf16).T)
        error = (
            coef * live_wide[None, :] * (recon_full - targets[t].T.astype(f32))
        ).astype(bf16)
        errors.append(jnp.sum(error.astype(f32), axis=1))
        outgoing = jnp.einsum(
            "di,ri->dr", error, place, preferred_element_type=f32
        ).astype(bf16)
        part = lax.all_to_all(outgoing, "expert", split_axis=1, concat_axis=1, tiled=True)
        segments.append(lax.all_gather(part, "layer", axis=0, tiled=True))
    recon = jnp.stack(recons)
    error_sums = lax.all_gather(jnp.stack(errors), ("expert", "dp"), axis=0)
    grad_b_dec = jnp.sum(error_sums, axis=0)

    grad_lat = sum(
        jnp.einsum("dr,ld->rl", segments[t], w_dec[t, 0], preferred_element_type=f32)
        for t in range(targets_count)
    )
    dec_parts = [
        lax.psum_scatter(
            jnp.einsum(
                "rl,hdr->hld",
                latents,
                segments[t].reshape(n_dp, model_width // n_dp, total_cells),
                preferred_element_type=f32,
            ).astype(bf16),
            "dp",
            scatter_dimension=0,
            tiled=True,
        )
        for t in range(targets_count)
    ]
    grad_pre = (grad_lat * (2.0 * active)).astype(bf16)
    grad_enc = jnp.einsum("dr,rl->dl", arrived, grad_pre, preferred_element_type=f32)
    enc_share = lax.psum_scatter(
        grad_enc.astype(bf16), "dp", scatter_dimension=0, tiled=True
    )
    grad_bias = jnp.sum(lax.optimization_barrier(grad_pre).astype(f32), axis=0)
    bias_share = lax.psum_scatter(grad_bias, "dp", scatter_dimension=0, tiled=True)
    return (recon, enc_share[None], bias_share[None], jnp.stack(dec_parts), grad_b_dec)


def solution(mesh):
    placed = (
        P(("expert", "dp"), None),
        P(("expert", "dp")),
        P(("expert", "dp")),
        P(("expert", "dp")),
        P("expert", None, "layer"),
        P("expert", "layer"),
        P(None, "expert", "layer", None),
        P(None, "layer"),
        P(None, ("expert", "dp"), "layer"),
    )
    return jax.shard_map(
        local,
        mesh=mesh,
        in_specs=placed,
        out_specs=(
            P(None, ("expert", "dp"), "layer"),
            P("expert", "dp", "layer"),
            P("expert", ("layer", "dp")),
            P(None, "expert", "layer", "dp"),
            P(None, "layer"),
        ),
        check_vma=False,
    )
```

time: 430 us -> 331 us (0.77)
  local copies, waits for them, and re-layouts: 80 us -> 22.7 us
  blocking collectives: 109 us -> 74.3 us
  waiting for transfers between devices: 189 us -> 163 us
  matrix products: 24.3 us -> 38.3 us
  starting transfers between devices: 4.94 us -> 9.79 us
    unnamed x7 -> x10, waiting for transfers between devices: 110 us -> 62.1 us
    all_to_all x2 -> x3, blocking collectives: 91.9 us -> 57.7 us  [the longest x2 35.7 us: local(): lax.all_to_all(outgoing, 'expert', split_axis=1, concat_axis=1, tiled=True)]
    all_gather x1 -> x3, waiting for transfers between devices: 55 us -> 87.9 us  [the longest x2 51.4 us: local(): segments.append(lax.all_gather(part, 'layer', axis=0, tiled=True))]
    scatter x2 -> x0, local copies, waits for them, and re-layouts: 31.9 us -> none  [place_rows(): return zero_fill.at[..., cell_index, :].set(values)]
    psum x1 -> x0, blocking collectives: 17 us -> none  [local(): grad_b_dec = lax.psum(jnp.sum(error_wide, axis=1), ('expert', 'dp'))]
    all_gather x0 -> x1, blocking collectives: none -> 14.1 us  [local(): error_sums = lax.all_gather(jnp.stack(errors), ('expert', 'dp'), axis=0)]
    dot_general x5 -> x13, matrix products: 24.3 us -> 38.3 us  [the longest x2 8.93 us: local(): jnp.einsum('rl,hdr->hld', latents, segments[t].reshape(n_dp, model_width...]
    optimization_barrier x1 -> x0, local copies, waits for them, and re-layouts: 12.4 us -> none  [local(): lax.optimization_barrier(partials).astype(jnp.float32).astype(jnp.bfloat16)]
  transfers between devices with their start and end apart: 6 -> 10, of which waited for: 3 -> 6; matrix products, arithmetic and copies ran while one was open for 6% -> 15% of each run, Pallas kernels for 0% -> 0%
where the time goes in v1:
time: 331 us; the launch traced here: 330 us
  waiting for transfers between devices  163 us (49%)
  blocking collectives  74.3 us (22%)
  matrix products  38.3 us (12%)
  local copies, waits for them, and re-layouts  22.7 us (7%)
  between operations  15 us (5%)
  starting transfers between devices  9.79 us (3%)
  other arithmetic  6.98 us (2%)
    unnamed x10, waiting for transfers between devices  62.1 us
    all_gather x2, waiting for transfers between devices, local(): segments.append(lax.all_gather(part, 'layer', axis=0, tiled=True))  51.4 us
    all_gather x1, waiting for transfers between devices, local(): arrived = lax.all_gather(arrived_part, 'layer', axis=0, tiled=True)  36.6 us
    all_to_all x2, blocking collectives, local(): lax.all_to_all(outgoing, 'expert', split_axis=1, concat_axis=1, tiled=True)  35.7 us
    all_to_all x1, blocking collectives, local(): lax.all_to_all(own, 'expert', split_axis=1, concat_axis=1, tiled=True)  22 us
    unnamed x33, local copies, waits for them, and re-layouts  17.6 us
    all_gather x1, blocking collectives, local(): error_sums = lax.all_gather(jnp.stack(errors), ('expert', 'dp'), axis=0)  14.1 us
    all_to_all x2, waiting for transfers between devices, local(): lax.all_to_all(summed[t], 'expert', split_axis=1, concat_axis=1, tiled=True)  12.9 us
  transfers between devices with their start and end apart: 10, of which 6 were waited for; matrix products, arithmetic and copies ran while one was open for 15% of the time, Pallas kernels for 0%

profile of v1, /device:TPU:0, one launch (start us, length us, event | category | flops | bytes accessed | tf_op | source)
XLA Modules:
  0.0 330.0 jit_solution(5153090965938535508)
XLA Ops:
  7.2 0.0 copy-start
  7.2 0.0 all-gather.6.cloned.1.call-start
  7.2 0.8 multiply_add_fusion
  8.1 2.1 fusion.46
  10.2 0.1 copy_bitcast_fusion.5
  10.3 22.0 %all_to_all.60 = bf16[576,4,128]{2,0,1:T(8,128)(2,1)S(1)} all-to-all(bf16[576,4,128]{2,0,1:T(8,128)(2,1)S(1)} %copy_bitcast_fusion.5), channel_id=1, replica_groups=mesh['layer'=4,'expert'=4,'dp'=2] {'expert'}, dimensions={1} | all-to-all | bytes 1179648 | tf_op jit(solution)/shard_map/all_to_all | solution.py:29
  32.4 0.9 copy_bitcast_fusion.2
  33.3 0.0 all-gather.6.cloned.1.call-update
  33.3 0.0 reduce-scatter.18.cloned.1.call-start
  33.3 36.6 %all-gather.6.cloned.1.call-done = bf16[2304,512]{1,0:T(8,128)(2,1)} async-done(((bf16[576,512]{1,0:T(8,128)(2,1)}), bf16[2304,512]{1,0:T(8,128)(2,1)}) %all-gather.6.cloned.1.call-update) | async-done | bytes 2359312 | tf_op jit(solution)/shard_map/all_gather | solution.py:30
  69.9 4.2 %multiply_convert_fusion = (bf16[512,512]{1,0:T(8,128)(2,1)S(1)}, f32[512,512]{1,0:T(8,128)}) fusion(f32[512]{0:T(512)S(1)} %bitcast.157, bf16[2304,512]{1,0:T(8,128)(2,1)} %all-gather.6.cloned.1.call-done, bf16[1,2304,512]{2,1,0:T(8,128)(2,1)S(1)} %copy-done), kind=kOutput, calls=%fused_computation.35 | convolution fusion | flops 1209008128 | bytes 6293504 | tf_op jit(solution)/shard_map/dr,dl->rl/dot_general | solution.py:31
  74.1 2.8 fusion.1
  76.9 4.3 %copy.34 = bf16[2304,512]{1,0:T(8,128)(2,1)} copy(bf16[2304,512]{0,1:T(8,128)(2,1)} %fusion.1) | data formatting | bytes 4718592
  81.2 0.0 reduce-scatter.18.cloned.1.call-update
  81.2 0.0 reduce-scatter.16.cloned.1.call-start
  81.3 4.5 %fusion = bf16[2304,512]{0,1:T(8,128)(2,1)} fusion(bf16[512,512]{1,0:T(8,128)(2,1)S(1)} %get-tuple-element.30, bf16[2,1,512,2304]{3,2,1,0:T(8,128)(2,1)} %param.15), kind=kOutput, calls=%fused_computation.3 | convolution fusion | flops 1209139200 | bytes 5242880 | tf_op jit(solution)/shard_map/ld,rl->dr/dot_general | solution.py:39
  85.8 4.3 %copy.32 = bf16[2304,512]{1,0:T(8,128)(2,1)} copy(bf16[2304,512]{0,1:T(8,128)(2,1)} %fusion) | data formatting | bytes 4718592
  90.1 0.0 reduce-scatter.16.cloned.1.call-update
  90.1 28.7 %reduce-scatter.18.cloned.1.call-done = bf16[576,512]{1,0:T(8,128)(2,1)} async-done(((bf16[2304,512]{1,0:T(8,128)(2,1)}), bf16[576,512]{1,0:T(8,128)(2,1)}) %reduce-scatter.18.cloned.1.call-update) | async-done | bytes 589840
  118.8 1.4 copy.35
  120.1 1.1 copy.25
  121.2 4.7 %all-to-all-start.2 = ((bf16[576,4,128]{2,0,1:T(8,128)(2,1)}), bf16[576,4,128]{2,0,1:T(8,128)(2,1)}, u32[]{:S(2)}, u32[]{:S(2)}) async-start(bf16[576,4,128]{2,0,1:T(8,128)(2,1)} %copy.25), calls=%async_computation.2 | async-start | bytes 1179648 | tf_op jit(solution)/shard_map/all_to_all | solution.py:47
  125.9 33.3 %reduce-scatter.16.cloned.1.call-done = bf16[576,512]{1,0:T(8,128)(2,1)} async-done(((bf16[2304,512]{1,0:T(8,128)(2,1)}), bf16[576,512]{1,0:T(8,128)(2,1)}) %reduce-scatter.16.cloned.1.call-update) | async-done | bytes 589840
  159.2 1.4 copy.33
  160.6 1.1 copy.23
  161.7 4.6 %all-to-all-start.1 = ((bf16[576,4,128]{2,0,1:T(8,128)(2,1)}), bf16[576,4,128]{2,0,1:T(8,128)(2,1)S(1)}, u32[]{:S(2)}, u32[]{:S(2)}) async-start(bf16[576,4,128]{2,0,1:T(8,128)(2,1)} %copy.23), calls=%async_computation.1 | async-start | bytes 1179648 | tf_op jit(solution)/shard_map/all_to_all | solution.py:47
  166.3 0.6 convert_multiply_fusion
  166.9 2.3 convolution_add_fusion
  169.1 12.9 %all-to-all-done.1 = bf16[576,4,128]{2,0,1:T(8,128)(2,1)S(1)} async-done(((bf16[576,4,128]{2,0,1:T(8,128)(2,1)}), bf16[576,4,128]{2,0,1:T(8,128)(2,1)S(1)}, u32[]{:S(2)}, u32[]{:S(2)}) %all-to-all-start.1) | async-done | bytes 589856 | tf_op jit(solution)/shard_map/all_to_all | solution.py:47
  182.0 2.7 convert_reduce_fusion.2
  184.7 0.4 fusion.31
  185.1 0.1 copy.61
  185.2 17.8 %all_to_all.61 = bf16[576,4,128]{2,0,1:T(8,128)(2,1)S(1)} all-to-all(bf16[576,4,128]{2,0,1:T(8,128)(2,1)S(1)} %bitcast.147), channel_id=1, replica_groups=mesh['layer'=4,'expert'=4,'dp'=2] {'expert'}, dimensions={1} | all-to-all | bytes 1179648 | tf_op jit(solution)/shard_map/all_to_all | solution.py:58
  203.0 0.9 copy_bitcast_fusion.1
  203.9 0.0 all-gather.8.cloned.1.call-update
  203.9 0.0 all-gather.10.cloned.1.call-start
  204.0 0.4 fusion.32
  204.4 0.1 copy.60
  204.5 17.8 %all_to_all.62 = bf16[576,4,128]{2,0,1:T(8,128)(2,1)S(1)} all-to-all(bf16[576,4,128]{2,0,1:T(8,128)(2,1)S(1)} %bitcast.148), channel_id=1, replica_groups=mesh['layer'=4,'expert'=4,'dp'=2] {'expert'}, dimensions={1} | all-to-all | bytes 1179648 | tf_op jit(solution)/shard_map/all_to_all | solution.py:58
  222.3 0.9 copy_bitcast_fusion
  223.2 0.0 all-gather.10.cloned.1.call-update
  223.2 0.0 reduce-scatter.12.cloned.1.call-start
  223.3 16.3 %all-gather.8.cloned.1.call-done = bf16[2304,512]{1,0:T(8,128)(2,1)} async-done(((bf16[576,512]{1,0:T(8,128)(2,1)}), bf16[2304,512]{1,0:T(8,128)(2,1)}) %all-gather.8.cloned.1.call-update) | async-done | bytes 2359312 | tf_op jit(solution)/shard_map/all_gather | solution.py:59
  239.6 4.5 %fusion.2 = bf16[2,512,1152]{1,2,0:T(8,128)(2,1)} fusion(bf16[2,1152,512]{2,1,0:T(8,128)(2,1)} %bitcast.154, bf16[512,512]{1,0:T(8,128)(2,1)S(1)} %copy-done.10), kind=kOutput, calls=%fused_computation.7 | convolution fusion | flops 1209139200 | bytes 5242880 | tf_op jit(solution)/shard_map/rl,hdr->hld/dot_general | solution.py:70
  244.0 0.0 reduce-scatter.12.cloned.1.call-update
  244.1 0.0 reduce-scatter.14.cloned.1.call-start
  244.1 35.1 %all-gather.10.cloned.1.call-done = bf16[2304,512]{1,0:T(8,128)(2,1)} async-done(((bf16[576,512]{1,0:T(8,128)(2,1)}), bf16[2304,512]{1,0:T(8,128)(2,1)}) %all-gather.10.cloned.1.call-update) | async-done | bytes 2359312 | tf_op jit(solution)/shard_map/all_gather | solution.py:59
  279.2 4.5 %fusion.3 = bf16[2,512,1152]{1,2,0:T(8,128)(2,1)} fusion(bf16[2,1152,512]{2,1,0:T(8,128)(2,1)} %bitcast.155, bf16[512,512]{1,0:T(8,128)(2,1)S(1)} %copy-done.10), kind=kOutput, calls=%fused_computation.8 | convolution fusion | flops 1209139200 | bytes 5242880 | tf_op jit(solution)/shard_map/rl,hdr->hld/dot_general | solution.py:70
  283.7 0.0 reduce-scatter.14.cloned.1.call-update
  283.7 0.2 reduce-scatter.10.cloned.1.call-start
  283.9 4.0 %fusion.4 = f32[512,512]{1,0:T(8,128)S(1)} fusion(bf16[2304,512]{1,0:T(8,128)(2,1)} %all-gather.10.cloned.1.call-done, bf16[2,1,512,2304]{3,2,1,0:T(8,128)(2,1)} %param.15), kind=kOutput, calls=%fused_computation.10 | convolution fusion | flops 1207959552 | bytes 5767168 | tf_op jit(solution)/shard_map/dr,ld->rl/dot_general | solution.py:65
  287.9 3.3 fusion.28
  291.2 2.9 convolution_convert_fusion
  294.1 0.0 reduce-scatter.10.cloned.1.call-update
  294.1 0.6 copy-done.7
  294.7 0.6 dynamic-slice.4
  296.0 14.1 %all-gather.1 = f32[8,2,576]{2,1,0:T(2,128)S(1)} all-gather(f32[1,2,576]{2,1,0:T(2,128)S(1)} %maximum_bitcast_fusion), channel_id=2, replica_groups=mesh['layer'=4,'expert'=4,'dp'=2] {'expert','dp'}, dimensions={0}, use_global_device_ids=true | all-gather | bytes 41472 | tf_op jit(solution)/shard_map/all_gather | solution.py:61
  310.1 0.6 reduce_sum.39
  310.8 0.9 pad_maximum_fusion.1
  311.6 0.1 convert_reduce_fusion
  311.7 2.5 all-reduce
  314.2 0.6 dynamic-slice.5
  314.9 4.0 %pad_maximum_fusion = bf16[2,1,512,1152]{2,3,1,0:T(8,128)(2,1)} fusion(bf16[1,1,512,1152]{2,3,1,0:T(8,128)(2,1)} %bitcast.150, bf16[1,1,512,1152]{2,3,1,0:T(8,128)(2,1)} %bitcast.149), kind=kLoop, calls=%fused_computation.9 | loop fusion | flops 1179648 | bytes 4718592 | tf_op jit(solution)/shard_map/stack | solution.py:89
  318.8 4.3 %copy.31 = bf16[2,1,512,1152]{3,2,1,0:T(8,128)(2,1)} copy(bf16[2,1,512,1152]{2,3,1,0:T(8,128)(2,1)} %pad_maximum_fusion) | data formatting | bytes 4718592
  (34 shorter events, 0.1 us)
Async XLA Ops:
  7.2 62.7 %copy-start = (bf16[1,2304,512]{2,1,0:T(8,128)(2,1)S(1)}, bf16[1,2304,512]{2,1,0:T(8,128)(2,1)}, u32[]{:S(2)}) copy-start(bf16[1,2304,512]{2,1,0:T(8,128)(2,1)} %param.13) | copy-start | bytes 7077892
  7.2 62.7 %all-gather.6.cloned.1.call-start = ((), (), s32[]{:S(2)}) async-start(), calls=%async_computation.10 | async-start | bytes 2949120 | tf_op jit(solution)/shard_map/all_gather | solution.py:30
  10.2 59.7 %copy-start.6 = (f32[1,512]{1,0:T(1,128)S(1)}, f32[1,512]{1,0:T(1,128)}, u32[]{:S(2)}) copy-start(f32[1,512]{1,0:T(1,128)} %param.14) | copy-start | bytes 6148
  33.3 40.8 %slice-start = ((s8[4718592]{0:T(1024)(128)(4,1)}), s8[524288]{0:T(1024)(128)(4,1)S(1)}, s32[]{:S(2)}) async-start(s8[4718592]{0:T(1024)(128)(4,1)} %bitcast.152), calls=%async_computation.18 | async-start | bytes 1048576
  33.3 85.5 %reduce-scatter.18.cloned.1.call-start = ((), (), s32[]{:S(2)}) async-start(), calls=%async_computation.17 | async-start | bytes 2949120
  69.9 4.2 %slice-start.1 = ((s8[4718592]{0:T(1024)(128)(4,1)}), s8[4194304]{0:T(1024)(128)(4,1)S(1)}, s32[]{:S(2)}) async-start(s8[4718592]{0:T(1024)(128)(4,1)} %bitcast.152), calls=%async_computation.19 | async-start | bytes 8388608
  74.1 7.2 %copy-start.9 = (bf16[512,512]{1,0:T(8,128)(2,1)}, bf16[512,512]{1,0:T(8,128)(2,1)S(1)}, u32[]{:S(2)}) copy-start(bf16[512,512]{1,0:T(8,128)(2,1)S(1)} %get-tuple-element.30) | copy-start | bytes 1572868
  81.2 78.0 %reduce-scatter.16.cloned.1.call-start = ((), (), s32[]{:S(2)}) async-start(), calls=%async_computation.16 | async-start | bytes 2949120
  121.2 45.1 %copy-start.2 = (f32[2,576]{1,0:T(2,128)S(1)}, f32[2,576]{1,0:T(2,128)}, u32[]{:S(2)}) copy-start(f32[2,576]{1,0:T(2,128)} %param.16) | copy-start | bytes 13828
  121.2 45.1 %copy-start.3 = (s32[256]{0:T(256)S(1)}, s32[256]{0:T(256)}, u32[]{:S(2)}) copy-start(s32[256]{0:T(256)} %param.12) | copy-start | bytes 3076
  121.2 40.5 %all-to-all-start.2 = ((bf16[576,4,128]{2,0,1:T(8,128)(2,1)}), bf16[576,4,128]{2,0,1:T(8,128)(2,1)}, u32[]{:S(2)}, u32[]{:S(2)}) async-start(bf16[576,4,128]{2,0,1:T(8,128)(2,1)} %copy.25), calls=%async_computation.2 | async-start | bytes 1179648 | tf_op jit(solution)/shard_map/all_to_all | solution.py:47
  161.7 20.3 %all-to-all-start.1 = ((bf16[576,4,128]{2,0,1:T(8,128)(2,1)}), bf16[576,4,128]{2,0,1:T(8,128)(2,1)S(1)}, u32[]{:S(2)}, u32[]{:S(2)}) async-start(bf16[576,4,128]{2,0,1:T(8,128)(2,1)} %copy.23), calls=%async_computation.1 | async-start | bytes 1179648 | tf_op jit(solution)/shard_map/all_to_all | solution.py:47
  166.3 73.3 %all-gather.8.cloned.1.call-start = ((), (), s32[]{:S(2)}) async-start(), calls=%async_computation.11 | async-start | bytes 2949120 | tf_op jit(solution)/shard_map/all_gather | solution.py:59
  184.7 19.3 %copy-start.1 = (bf16[576,256]{1,0:T(8,128)(2,1)S(1)}, bf16[576,256]{1,0:T(8,128)(2,1)}, u32[]{:S(2)}) copy-start(bf16[576,256]{1,0:T(8,128)(2,1)} %get-tuple-element.27) | copy-start | bytes 884740
  203.9 75.3 %all-gather.10.cloned.1.call-start = ((), (), s32[]{:S(2)}) async-start(), calls=%async_computation.12 | async-start | bytes 2949120 | tf_op jit(solution)/shard_map/all_gather | solution.py:59
  204.4 35.2 %copy-start.10 = (bf16[512,512]{1,0:T(8,128)(2,1)S(1)}, bf16[512,512]{1,0:T(8,128)(2,1)}, u32[]{:S(2)}) copy-start(bf16[512,512]{1,0:T(8,128)(2,1)} %copy-done.9) | copy-start | bytes 1572868
  223.2 91.6 %reduce-scatter.12.cloned.1.call-start = ((), (), s32[]{:S(2)}) async-start(), calls=%async_computation.14 | async-start | bytes 3538944 | tf_op jit(solution)/shard_map/reduce_scatter | solution.py:69
  244.1 70.8 %reduce-scatter.14.cloned.1.call-start = ((), (), s32[]{:S(2)}) async-start(), calls=%async_computation.15 | async-start | bytes 3538944 | tf_op jit(solution)/shard_map/reduce_scatter | solution.py:69
  283.7 39.5 %reduce-scatter.10.cloned.1.call-start = ((), (), s32[]{:S(2)}) async-start(), calls=%async_computation.13 | async-start | bytes 3538944 | tf_op jit(solution)/shard_map/reduce_scatter | solution.py:84
  283.9 4.0 %copy-start.5 = (bf16[2304,512]{1,0:T(8,128)(2,1)S(1)}, bf16[2304,512]{1,0:T(8,128)(2,1)}, u32[]{:S(2)}) copy-start(bf16[2304,512]{1,0:T(8,128)(2,1)} %all-gather.8.cloned.1.call-done) | copy-start | bytes 7077892
  283.9 4.0 %copy-start.8 = (f32[512,512]{1,0:T(8,128)S(1)}, f32[512,512]{1,0:T(8,128)}, u32[]{:S(2)}) copy-start(f32[512,512]{1,0:T(8,128)} %get-tuple-element.31) | copy-start | bytes 3145732
  287.9 3.3 copy-start.4
  294.1 0.7 copy-start.7
Sparse Core Ops, SparseCore 0:
  33.4 36.4 all-gather.5
  81.4 37.3 reduce-scatter.17
  121.8 37.3 reduce-scatter.15
  204.1 35.4 all-gather.7
  241.8 37.3 all-gather.9
  281.3 10.0 reduce-scatter.11
  294.3 11.3 reduce-scatter.13
  308.5 11.3 reduce-scatter.9
